TPU v7x, 32 devices: a whole 2x2x4 slice. The times are simulated.
32 devices in a mesh: row: 8 (over y, x, core), feat: 4 (over z).
Axes of the slice: x: 2, y: 2, z: 4, core: 2. Of those that a mesh axis runs over, the one named last changes fastest.
Arguments:
- bins: int32 [1024, 65536], P('feat', 'row'), may hold values from 0 to 255
- grads: bfloat16 [65536], P('row'), may hold values from -6 to 6
- hess: bfloat16 [65536], P('row'), may hold values from 0.049804688 to 1
- node: int32 [65536], P('row'), may hold values from 0 to 7
Outputs:
- shortfall: float32 [1024, 8, 256], P(('feat', 'row'))
- best: float32 [8], replicated
All inputs are finite; a program needn't handle non-finite values.
Results may differ from a plain program's by a relative error of at most 0.0003.
Values sent between devices are 32-bit elements; how exact they have to be, the bound alone decides.
A program may use at most 64 MiB of HBM per device.

v0:
```python
import jax
import jax.numpy as jnp
from jax import lax
from jax.sharding import PartitionSpec as P

BINS = 256
NODES = 8


def per_device(bins, grads, hess, node):
    feat_local = bins.shape[0]
    row_count = bins.shape[1]
    member = node[None, :] == jnp.arange(NODES, dtype=jnp.int32)[:, None]
    zero = jnp.zeros((), jnp.bfloat16)
    weighted = jnp.concatenate(
        [jnp.where(member, grads[None, :], zero), jnp.where(member, hess[None, :], zero)], axis=0
    )
    own_sums = jnp.sum(weighted.astype(jnp.float32), axis=1)
    node_sums = lax.psum(own_sums, "row")
    blocks = bins.reshape(feat_local // 8, 8, row_count)
    levels = jnp.arange(BINS, dtype=jnp.int32)

    def block_hist(columns):
        onehot = (columns[:, :, None] == levels[None, None, :]).astype(jnp.bfloat16)
        return jnp.einsum("kr,frb->fkb", weighted, onehot, preferred_element_type=jnp.float32)

    partial_hist = lax.map(block_hist, blocks).reshape(feat_local, 2 * NODES, BINS)
    hist = lax.psum_scatter(partial_hist, "row", scatter_dimension=0, tiled=True)
    grad_total = node_sums[None, :NODES, None]
    hess_total = node_sums[None, NODES:, None]
    left = jnp.cumsum(hist, axis=2)
    grad_left = left[:, :NODES]
    hess_left = left[:, NODES:]
    gain = grad_left * grad_left / (hess_left + 1.0)
    gain = gain + (grad_total - grad_left) ** 2 / (hess_total - hess_left + 1.0)
    gain = gain - grad_total * grad_total / (hess_total + 1.0)
    local_best = jnp.max(gain, axis=(0, 2))
    best = lax.pmax(local_best, ("row", "feat"))
    return (gain - best[None, :, None], best)


def solution(mesh):
    return jax.shard_map(
        per_device,
        mesh=mesh,
        in_specs=(P("feat", "row"), P("row"), P("row"), P("row")),
        out_specs=(P(("feat", "row"), None, None), P()),
        check_vma=False,
    )
```

profile of v0, /device:TPU:0, one launch (start us, length us, event | category | flops | bytes accessed | tf_op | source)
XLA Modules:
  0.0 560.5 jit_solution(14059853241810017345)
XLA Ops:
  8.1 431.1 %while.11 = (s32[]{:T(128)}, f32[32,8,16,256]{3,2,1,0:T(8,128)}, s32[32,8,8192]{2,1,0:T(8,128)}, bf16[16,8192]{1,0:T(8,128)(2,1)S(1)}, s32[]{:T(128)}) while((s32[]{:T(128)}, f32[32,8,16,256]{3,2,1,0:T(8,128)}, s32[32,8,8192]{2,1,0:T(8,128)}, bf16[16,8192]{1,0:T(8,128)(2,1)S(1)}, s32[]{:T(128)}) %tuple.34), condition=%wide.region_1.2_spmd.clone, body=%wide.region_0.1_spmd.clone.sunk | while | flops 553648128 | bytes 1179725 | solution.py:27
  9.1 12.5 %fusion.18 = f32[32,8,16,256]{3,2,1,0:T(8,128)} fusion(f32[32,8,16,256]{3,2,1,0:T(8,128)} %get-tuple-element.86, s32[]{:T(128)S(6)} %copy.17, s32[8,8192]{1,0:T(8,128)S(1)} %dynamic-slice_bitcast_fusion.2, bf16[16,8192]{1,0:T(8,128)(2,1)S(1)} %get-tuple-element.93), kind=kOutput, calls=%fused_computation.5.clone.2 | convolution fusion | flops 553648128 | bytes 655364 | tf_op jit(solution)/shard_map/while/body/eval_jaxpr/kr,frb->fkb/dot_general | solution.py:25
  22.5 12.5 %fusion.18 = f32[32,8,16,256]{3,2,1,0:T(8,128)} fusion(f32[32,8,16,256]{3,2,1,0:T(8,128)} %get-tuple-element.86, s32[]{:T(128)S(6)} %copy.17, s32[8,8192]{1,0:T(8,128)S(1)} %dynamic-slice_bitcast_fusion.2, bf16[16,8192]{1,0:T(8,128)(2,1)S(1)} %get-tuple-element.93), kind=kOutput, calls=%fused_computation.5.clone.2 | convolution fusion | flops 553648128 | bytes 655364 | tf_op jit(solution)/shard_map/while/body/eval_jaxpr/kr,frb->fkb/dot_general | solution.py:25
  36.0 12.5 %fusion.18 = f32[32,8,16,256]{3,2,1,0:T(8,128)} fusion(f32[32,8,16,256]{3,2,1,0:T(8,128)} %get-tuple-element.86, s32[]{:T(128)S(6)} %copy.17, s32[8,8192]{1,0:T(8,128)S(1)} %dynamic-slice_bitcast_fusion.2, bf16[16,8192]{1,0:T(8,128)(2,1)S(1)} %get-tuple-element.93), kind=kOutput, calls=%fused_computation.5.clone.2 | convolution fusion | flops 553648128 | bytes 655364 | tf_op jit(solution)/shard_map/while/body/eval_jaxpr/kr,frb->fkb/dot_general | solution.py:25
  49.5 12.5 %fusion.18 = f32[32,8,16,256]{3,2,1,0:T(8,128)} fusion(f32[32,8,16,256]{3,2,1,0:T(8,128)} %get-tuple-element.86, s32[]{:T(128)S(6)} %copy.17, s32[8,8192]{1,0:T(8,128)S(1)} %dynamic-slice_bitcast_fusion.2, bf16[16,8192]{1,0:T(8,128)(2,1)S(1)} %get-tuple-element.93), kind=kOutput, calls=%fused_computation.5.clone.2 | convolution fusion | flops 553648128 | bytes 655364 | tf_op jit(solution)/shard_map/while/body/eval_jaxpr/kr,frb->fkb/dot_general | solution.py:25
  76.4 12.5 %fusion.18 = f32[32,8,16,256]{3,2,1,0:T(8,128)} fusion(f32[32,8,16,256]{3,2,1,0:T(8,128)} %get-tuple-element.86, s32[]{:T(128)S(6)} %copy.17, s32[8,8192]{1,0:T(8,128)S(1)} %dynamic-slice_bitcast_fusion.2, bf16[16,8192]{1,0:T(8,128)(2,1)S(1)} %get-tuple-element.93), kind=kOutput, calls=%fused_computation.5.clone.2 | convolution fusion | flops 553648128 | bytes 655364 | tf_op jit(solution)/shard_map/while/body/eval_jaxpr/kr,frb->fkb/dot_general | solution.py:25
  89.9 12.5 %fusion.18 = f32[32,8,16,256]{3,2,1,0:T(8,128)} fusion(f32[32,8,16,256]{3,2,1,0:T(8,128)} %get-tuple-element.86, s32[]{:T(128)S(6)} %copy.17, s32[8,8192]{1,0:T(8,128)S(1)} %dynamic-slice_bitcast_fusion.2, bf16[16,8192]{1,0:T(8,128)(2,1)S(1)} %get-tuple-element.93), kind=kOutput, calls=%fused_computation.5.clone.2 | convolution fusion | flops 553648128 | bytes 655364 | tf_op jit(solution)/shard_map/while/body/eval_jaxpr/kr,frb->fkb/dot_general | solution.py:25
  103.4 12.5 %fusion.18 = f32[32,8,16,256]{3,2,1,0:T(8,128)} fusion(f32[32,8,16,256]{3,2,1,0:T(8,128)} %get-tuple-element.86, s32[]{:T(128)S(6)} %copy.17, s32[8,8192]{1,0:T(8,128)S(1)} %dynamic-slice_bitcast_fusion.2, bf16[16,8192]{1,0:T(8,128)(2,1)S(1)} %get-tuple-element.93), kind=kOutput, calls=%fused_computation.5.clone.2 | convolution fusion | flops 553648128 | bytes 655364 | tf_op jit(solution)/shard_map/while/body/eval_jaxpr/kr,frb->fkb/dot_general | solution.py:25
  116.8 12.5 %fusion.18 = f32[32,8,16,256]{3,2,1,0:T(8,128)} fusion(f32[32,8,16,256]{3,2,1,0:T(8,128)} %get-tuple-element.86, s32[]{:T(128)S(6)} %copy.17, s32[8,8192]{1,0:T(8,128)S(1)} %dynamic-slice_bitcast_fusion.2, bf16[16,8192]{1,0:T(8,128)(2,1)S(1)} %get-tuple-element.93), kind=kOutput, calls=%fused_computation.5.clone.2 | convolution fusion | flops 553648128 | bytes 655364 | tf_op jit(solution)/shard_map/while/body/eval_jaxpr/kr,frb->fkb/dot_general | solution.py:25
  130.3 12.5 %fusion.18 = f32[32,8,16,256]{3,2,1,0:T(8,128)} fusion(f32[32,8,16,256]{3,2,1,0:T(8,128)} %get-tuple-element.86, s32[]{:T(128)S(6)} %copy.17, s32[8,8192]{1,0:T(8,128)S(1)} %dynamic-slice_bitcast_fusion.2, bf16[16,8192]{1,0:T(8,128)(2,1)S(1)} %get-tuple-element.93), kind=kOutput, calls=%fused_computation.5.clone.2 | convolution fusion | flops 553648128 | bytes 655364 | tf_op jit(solution)/shard_map/while/body/eval_jaxpr/kr,frb->fkb/dot_general | solution.py:25
  143.8 12.5 %fusion.18 = f32[32,8,16,256]{3,2,1,0:T(8,128)} fusion(f32[32,8,16,256]{3,2,1,0:T(8,128)} %get-tuple-element.86, s32[]{:T(128)S(6)} %copy.17, s32[8,8192]{1,0:T(8,128)S(1)} %dynamic-slice_bitcast_fusion.2, bf16[16,8192]{1,0:T(8,128)(2,1)S(1)} %get-tuple-element.93), kind=kOutput, calls=%fused_computation.5.clone.2 | convolution fusion | flops 553648128 | bytes 655364 | tf_op jit(solution)/shard_map/while/body/eval_jaxpr/kr,frb->fkb/dot_general | solution.py:25
  157.2 12.5 %fusion.18 = f32[32,8,16,256]{3,2,1,0:T(8,128)} fusion(f32[32,8,16,256]{3,2,1,0:T(8,128)} %get-tuple-element.86, s32[]{:T(128)S(6)} %copy.17, s32[8,8192]{1,0:T(8,128)S(1)} %dynamic-slice_bitcast_fusion.2, bf16[16,8192]{1,0:T(8,128)(2,1)S(1)} %get-tuple-element.93), kind=kOutput, calls=%fused_computation.5.clone.2 | convolution fusion | flops 553648128 | bytes 655364 | tf_op jit(solution)/shard_map/while/body/eval_jaxpr/kr,frb->fkb/dot_general | solution.py:25
  170.7 12.5 %fusion.18 = f32[32,8,16,256]{3,2,1,0:T(8,128)} fusion(f32[32,8,16,256]{3,2,1,0:T(8,128)} %get-tuple-element.86, s32[]{:T(128)S(6)} %copy.17, s32[8,8192]{1,0:T(8,128)S(1)} %dynamic-slice_bitcast_fusion.2, bf16[16,8192]{1,0:T(8,128)(2,1)S(1)} %get-tuple-element.93), kind=kOutput, calls=%fused_computation.5.clone.2 | convolution fusion | flops 553648128 | bytes 655364 | tf_op jit(solution)/shard_map/while/body/eval_jaxpr/kr,frb->fkb/dot_general | solution.py:25
  184.2 12.5 %fusion.18 = f32[32,8,16,256]{3,2,1,0:T(8,128)} fusion(f32[32,8,16,256]{3,2,1,0:T(8,128)} %get-tuple-element.86, s32[]{:T(128)S(6)} %copy.17, s32[8,8192]{1,0:T(8,128)S(1)} %dynamic-slice_bitcast_fusion.2, bf16[16,8192]{1,0:T(8,128)(2,1)S(1)} %get-tuple-element.93), kind=kOutput, calls=%fused_computation.5.clone.2 | convolution fusion | flops 553648128 | bytes 655364 | tf_op jit(solution)/shard_map/while/body/eval_jaxpr/kr,frb->fkb/dot_general | solution.py:25
  197.6 12.5 %fusion.18 = f32[32,8,16,256]{3,2,1,0:T(8,128)} fusion(f32[32,8,16,256]{3,2,1,0:T(8,128)} %get-tuple-element.86, s32[]{:T(128)S(6)} %copy.17, s32[8,8192]{1,0:T(8,128)S(1)} %dynamic-slice_bitcast_fusion.2, bf16[16,8192]{1,0:T(8,128)(2,1)S(1)} %get-tuple-element.93), kind=kOutput, calls=%fused_computation.5.clone.2 | convolution fusion | flops 553648128 | bytes 655364 | tf_op jit(solution)/shard_map/while/body/eval_jaxpr/kr,frb->fkb/dot_general | solution.py:25
  211.1 12.5 %fusion.18 = f32[32,8,16,256]{3,2,1,0:T(8,128)} fusion(f32[32,8,16,256]{3,2,1,0:T(8,128)} %get-tuple-element.86, s32[]{:T(128)S(6)} %copy.17, s32[8,8192]{1,0:T(8,128)S(1)} %dynamic-slice_bitcast_fusion.2, bf16[16,8192]{1,0:T(8,128)(2,1)S(1)} %get-tuple-element.93), kind=kOutput, calls=%fused_computation.5.clone.2 | convolution fusion | flops 553648128 | bytes 655364 | tf_op jit(solution)/shard_map/while/body/eval_jaxpr/kr,frb->fkb/dot_general | solution.py:25
  238.1 12.5 %fusion.18 = f32[32,8,16,256]{3,2,1,0:T(8,128)} fusion(f32[32,8,16,256]{3,2,1,0:T(8,128)} %get-tuple-element.86, s32[]{:T(128)S(6)} %copy.17, s32[8,8192]{1,0:T(8,128)S(1)} %dynamic-slice_bitcast_fusion.2, bf16[16,8192]{1,0:T(8,128)(2,1)S(1)} %get-tuple-element.93), kind=kOutput, calls=%fused_computation.5.clone.2 | convolution fusion | flops 553648128 | bytes 655364 | tf_op jit(solution)/shard_map/while/body/eval_jaxpr/kr,frb->fkb/dot_general | solution.py:25
  251.5 12.5 %fusion.18 = f32[32,8,16,256]{3,2,1,0:T(8,128)} fusion(f32[32,8,16,256]{3,2,1,0:T(8,128)} %get-tuple-element.86, s32[]{:T(128)S(6)} %copy.17, s32[8,8192]{1,0:T(8,128)S(1)} %dynamic-slice_bitcast_fusion.2, bf16[16,8192]{1,0:T(8,128)(2,1)S(1)} %get-tuple-element.93), kind=kOutput, calls=%fused_computation.5.clone.2 | convolution fusion | flops 553648128 | bytes 655364 | tf_op jit(solution)/shard_map/while/body/eval_jaxpr/kr,frb->fkb/dot_general | solution.py:25
  265.0 12.5 %fusion.18 = f32[32,8,16,256]{3,2,1,0:T(8,128)} fusion(f32[32,8,16,256]{3,2,1,0:T(8,128)} %get-tuple-element.86, s32[]{:T(128)S(6)} %copy.17, s32[8,8192]{1,0:T(8,128)S(1)} %dynamic-slice_bitcast_fusion.2, bf16[16,8192]{1,0:T(8,128)(2,1)S(1)} %get-tuple-element.93), kind=kOutput, calls=%fused_computation.5.clone.2 | convolution fusion | flops 553648128 | bytes 655364 | tf_op jit(solution)/shard_map/while/body/eval_jaxpr/kr,frb->fkb/dot_general | solution.py:25
  278.5 12.5 %fusion.18 = f32[32,8,16,256]{3,2,1,0:T(8,128)} fusion(f32[32,8,16,256]{3,2,1,0:T(8,128)} %get-tuple-element.86, s32[]{:T(128)S(6)} %copy.17, s32[8,8192]{1,0:T(8,128)S(1)} %dynamic-slice_bitcast_fusion.2, bf16[16,8192]{1,0:T(8,128)(2,1)S(1)} %get-tuple-element.93), kind=kOutput, calls=%fused_computation.5.clone.2 | convolution fusion | flops 553648128 | bytes 655364 | tf_op jit(solution)/shard_map/while/body/eval_jaxpr/kr,frb->fkb/dot_general | solution.py:25
  305.4 12.5 %fusion.18 = f32[32,8,16,256]{3,2,1,0:T(8,128)} fusion(f32[32,8,16,256]{3,2,1,0:T(8,128)} %get-tuple-element.86, s32[]{:T(128)S(6)} %copy.17, s32[8,8192]{1,0:T(8,128)S(1)} %dynamic-slice_bitcast_fusion.2, bf16[16,8192]{1,0:T(8,128)(2,1)S(1)} %get-tuple-element.93), kind=kOutput, calls=%fused_computation.5.clone.2 | convolution fusion | flops 553648128 | bytes 655364 | tf_op jit(solution)/shard_map/while/body/eval_jaxpr/kr,frb->fkb/dot_general | solution.py:25
  332.3 12.5 %fusion.18 = f32[32,8,16,256]{3,2,1,0:T(8,128)} fusion(f32[32,8,16,256]{3,2,1,0:T(8,128)} %get-tuple-element.86, s32[]{:T(128)S(6)} %copy.17, s32[8,8192]{1,0:T(8,128)S(1)} %dynamic-slice_bitcast_fusion.2, bf16[16,8192]{1,0:T(8,128)(2,1)S(1)} %get-tuple-element.93), kind=kOutput, calls=%fused_computation.5.clone.2 | convolution fusion | flops 553648128 | bytes 655364 | tf_op jit(solution)/shard_map/while/body/eval_jaxpr/kr,frb->fkb/dot_general | solution.py:25
  345.8 12.5 %fusion.18 = f32[32,8,16,256]{3,2,1,0:T(8,128)} fusion(f32[32,8,16,256]{3,2,1,0:T(8,128)} %get-tuple-element.86, s32[]{:T(128)S(6)} %copy.17, s32[8,8192]{1,0:T(8,128)S(1)} %dynamic-slice_bitcast_fusion.2, bf16[16,8192]{1,0:T(8,128)(2,1)S(1)} %get-tuple-element.93), kind=kOutput, calls=%fused_computation.5.clone.2 | convolution fusion | flops 553648128 | bytes 655364 | tf_op jit(solution)/shard_map/while/body/eval_jaxpr/kr,frb->fkb/dot_general | solution.py:25
  359.3 12.5 %fusion.18 = f32[32,8,16,256]{3,2,1,0:T(8,128)} fusion(f32[32,8,16,256]{3,2,1,0:T(8,128)} %get-tuple-element.86, s32[]{:T(128)S(6)} %copy.17, s32[8,8192]{1,0:T(8,128)S(1)} %dynamic-slice_bitcast_fusion.2, bf16[16,8192]{1,0:T(8,128)(2,1)S(1)} %get-tuple-element.93), kind=kOutput, calls=%fused_computation.5.clone.2 | convolution fusion | flops 553648128 | bytes 655364 | tf_op jit(solution)/shard_map/while/body/eval_jaxpr/kr,frb->fkb/dot_general | solution.py:25
  372.8 12.5 %fusion.18 = f32[32,8,16,256]{3,2,1,0:T(8,128)} fusion(f32[32,8,16,256]{3,2,1,0:T(8,128)} %get-tuple-element.86, s32[]{:T(128)S(6)} %copy.17, s32[8,8192]{1,0:T(8,128)S(1)} %dynamic-slice_bitcast_fusion.2, bf16[16,8192]{1,0:T(8,128)(2,1)S(1)} %get-tuple-element.93), kind=kOutput, calls=%fused_computation.5.clone.2 | convolution fusion | flops 553648128 | bytes 655364 | tf_op jit(solution)/shard_map/while/body/eval_jaxpr/kr,frb->fkb/dot_general | solution.py:25
  399.7 12.5 %fusion.18 = f32[32,8,16,256]{3,2,1,0:T(8,128)} fusion(f32[32,8,16,256]{3,2,1,0:T(8,128)} %get-tuple-element.86, s32[]{:T(128)S(6)} %copy.17, s32[8,8192]{1,0:T(8,128)S(1)} %dynamic-slice_bitcast_fusion.2, bf16[16,8192]{1,0:T(8,128)(2,1)S(1)} %get-tuple-element.93), kind=kOutput, calls=%fused_computation.5.clone.2 | convolution fusion | flops 553648128 | bytes 655364 | tf_op jit(solution)/shard_map/while/body/eval_jaxpr/kr,frb->fkb/dot_general | solution.py:25
  413.2 12.5 %fusion.18 = f32[32,8,16,256]{3,2,1,0:T(8,128)} fusion(f32[32,8,16,256]{3,2,1,0:T(8,128)} %get-tuple-element.86, s32[]{:T(128)S(6)} %copy.17, s32[8,8192]{1,0:T(8,128)S(1)} %dynamic-slice_bitcast_fusion.2, bf16[16,8192]{1,0:T(8,128)(2,1)S(1)} %get-tuple-element.93), kind=kOutput, calls=%fused_computation.5.clone.2 | convolution fusion | flops 553648128 | bytes 655364 | tf_op jit(solution)/shard_map/while/body/eval_jaxpr/kr,frb->fkb/dot_general | solution.py:25
  426.6 12.5 %fusion.18 = f32[32,8,16,256]{3,2,1,0:T(8,128)} fusion(f32[32,8,16,256]{3,2,1,0:T(8,128)} %get-tuple-element.86, s32[]{:T(128)S(6)} %copy.17, s32[8,8192]{1,0:T(8,128)S(1)} %dynamic-slice_bitcast_fusion.2, bf16[16,8192]{1,0:T(8,128)(2,1)S(1)} %get-tuple-element.93), kind=kOutput, calls=%fused_computation.5.clone.2 | convolution fusion | flops 553648128 | bytes 655364 | tf_op jit(solution)/shard_map/while/body/eval_jaxpr/kr,frb->fkb/dot_general | solution.py:25
  439.3 15.1 %psum.7 = f32[16]{0:T(128)S(1)} all-reduce(f32[16]{0:T(128)S(1)} %convert_reduce_fusion), channel_id=1, replica_groups=mesh['row'=8,'feat'=4] {'row'}, use_global_device_ids=true, to_apply=%region_6.7 | all-reduce | flops 16 | bytes 128 | tf_op jit(solution)/shard_map/psum | solution.py:19
  454.6 38.6 %reduce-scatter.2.cloned.1.call-done = f32[32,16,256]{2,1,0:T(8,128)} async-done(((f32[256,16,256]{2,1,0:T(8,128)}), f32[32,16,256]{2,1,0:T(8,128)}) %reduce-scatter.2.cloned.1.call-update) | async-done | bytes 524304 | tf_op jit(solution)/shard_map/reduce_scatter | solution.py:28
  494.3 18.1 %reduce-window.6 = f32[32,16,2,128]{3,1,2,0:T(8,128)S(1)} reduce-window(f32[32,16,2,128]{3,1,2,0:T(8,128)S(1)} %copy_bitcast_fusion.1, f32[]{:T(128)} %constant.7.clone.1), window={size=1x1x1x128 pad=0_0x0_0x0_0x127_0}, to_apply=%region_3.4 | reduce-window | flops 16646144 | bytes 1048580 | tf_op jit(solution)/shard_map/reduce-window
  513.6 39.3 %pmax.7 = f32[8]{0:T(128)S(1)} all-reduce(f32[8]{0:T(128)S(1)} %get-tuple-element.48), channel_id=1, replica_groups=mesh['row'=8,'feat'=4] {'row','feat'}, use_global_device_ids=true, to_apply=%region_8.9 | all-reduce | flops 8 | bytes 64 | tf_op jit(solution)/shard_map/pmax | solution.py:38
  (55 shorter events, 97.6 us)
Async XLA Ops:
  7.2 486.0 %reduce-scatter.2.cloned.1.call-start = ((), (), s32[]{:S(2)}) async-start(), calls=%async_computation.1 | async-start | bytes 4718592 | tf_op jit(solution)/shard_map/reduce_scatter | solution.py:28
  552.9 0.8 copy-start
Sparse Core Ops, SparseCore 0:
  439.3 53.8 reduce-scatter.1
where the time goes:
time: 562 us; the launch traced here: 561 us
  matrix products  400 us (71%)
  blocking collectives  54.4 us (10%)
  waiting for transfers between devices  38.7 us (7%)
  local copies, waits for them, and re-layouts  32.7 us (6%)
  other arithmetic  20.6 us (4%)
  between operations  14.1 us (3%)
    dot_general x32, matrix products, block_hist(): jnp.einsum('kr,frb->fkb', weighted, onehot, preferred_element_type=jnp.fl...  400 us
    pmax x1, blocking collectives, per_device(): best = lax.pmax(local_best, ('row', 'feat'))  39.3 us
    reduce_scatter x1, waiting for transfers between devices, per_device(): lax.psum_scatter(partial_hist, 'row', scatter_dimension=0, tiled=True)  38.6 us
    eq x32, local copies, waits for them, and re-layouts, block_hist(): onehot = (columns[:, :, None] == levels[None, None, :]).astype(jnp.bfloat16)  30.9 us
    another operation x3, other arithmetic  18.4 us
    psum x1, blocking collectives, per_device(): node_sums = lax.psum(own_sums, 'row')  15.1 us
  transfers between devices with their start and end apart: 1, of which 1 were waited for; matrix products, arithmetic and copies ran while one was open for 0% of the time, Pallas kernels for 0%

commit v1 on v0

v1 whole, which is shorter than its diff:
```python
import functools
import jax
import jax.numpy as jnp
from jax import lax
from jax.experimental import pallas as pl
from jax.experimental.pallas import tpu as pltpu
from jax.sharding import PartitionSpec as P

BINS = 256
NODES = 8
LANES = 128
LOW = 64
TILE = 256
GROUP = TILE // LOW
HALVES = LANES // LOW
SLOTS = NODES * BINS // LANES


def hist_kernel(bins_ref, node_ref, g_ref, h_ref, out_ref, high_ref, low_ref, g_all, h_all, acc_ref):
    features, rows = bins_ref.shape

    @pl.when(pl.program_id(0) == 0)
    def _():
        g_all[...] = jnp.broadcast_to(g_ref[...], g_all.shape).astype(jnp.bfloat16)
        h_all[...] = jnp.broadcast_to(h_ref[...], h_all.shape).astype(jnp.bfloat16)

    bins = bins_ref[...]
    half = (bins // LOW) % HALVES
    slot = node_ref[...] * (BINS // LANES) + bins // LANES
    high_ref[...] = (half * SLOTS + slot).astype(jnp.float32)
    low_ref[...] = (bins % LOW).astype(jnp.float32)
    place = lax.broadcasted_iota(jnp.int32, (SLOTS, rows), 0).astype(jnp.bfloat16)
    zero = jnp.zeros((SLOTS, rows), jnp.bfloat16)
    one = jnp.ones((SLOTS, rows), jnp.bfloat16)
    for first in range(0, features, GROUP):
        left, right = [], []
        for f in range(first, first + GROUP):
            high = jnp.broadcast_to(high_ref[f : f + 1, :], (SLOTS, rows)).astype(jnp.bfloat16)
            low = jnp.broadcast_to(low_ref[f : f + 1, :], (SLOTS, rows)).astype(jnp.bfloat16)
            for j in range(HALVES):
                here = high == place + jnp.asarray(SLOTS * j, jnp.bfloat16)
                left += [jnp.where(here, g_all[...], zero), jnp.where(here, h_all[...], zero)]
            for j in range(LOW // SLOTS):
                here = low == place + jnp.asarray(SLOTS * j, jnp.bfloat16)
                right.append(jnp.where(here, one, zero))
        acc_ref[...] = lax.dot_general(
            jnp.concatenate(left, 0),
            jnp.concatenate(right, 0),
            (((1,), (1,)), ((), ())),
            preferred_element_type=jnp.float32,
        )
        for i in range(GROUP):
            parts = []
            for j in range(HALVES):
                top = (i * HALVES + j) * 2 * SLOTS
                parts.append(acc_ref[top : top + 2 * SLOTS, i * LOW : (i + 1) * LOW])
            out_ref[first + i] = jnp.concatenate(parts, 1)


def local_hist(bins, node, grads, hess, block):
    features, rows = bins.shape
    whole = pl.BlockSpec((1, rows), lambda i: (0, 0))
    return pl.pallas_call(
        hist_kernel,
        grid=(features // block,),
        in_specs=[pl.BlockSpec((block, rows), lambda i: (i, 0)), whole, whole, whole],
        out_specs=pl.BlockSpec((block, 2 * SLOTS, LANES), lambda i: (i, 0, 0)),
        out_shape=jax.ShapeDtypeStruct((features, 2 * SLOTS, LANES), jnp.float32),
        scratch_shapes=[
            pltpu.VMEM((block, rows), jnp.float32),
            pltpu.VMEM((block, rows), jnp.float32),
            pltpu.VMEM((SLOTS, rows), jnp.bfloat16),
            pltpu.VMEM((SLOTS, rows), jnp.bfloat16),
            pltpu.VMEM((GROUP * HALVES * 2 * SLOTS, TILE), jnp.float32),
        ],
        compiler_params=pltpu.CompilerParams(vmem_limit_bytes=56 << 20),
    )(bins, node, grads, hess)


def gain_kernel(hist_ref, gain_ref, best_ref):
    x = hist_ref[...]
    features = x.shape[0]
    x = x.reshape(features * 2 * SLOTS, LANES)
    lane = lax.broadcasted_iota(jnp.int32, x.shape, 1)
    step = 1
    while step < LANES:
        x = x + jnp.where(lane >= step, pltpu.roll(x, step, 1), 0.0)
        step *= 2
    row = lax.broadcasted_iota(jnp.int32, x.shape, 0)
    ends = jnp.broadcast_to(x[:, LANES - 1 :], x.shape)
    upper = row % 2 == 1
    n_rows = x.shape[0]
    left = x + jnp.where(upper, pltpu.roll(ends, 1, 0), 0.0)
    total = jnp.where(upper, pltpu.roll(ends, 1, 0), pltpu.roll(ends, n_rows - 1, 0)) + ends
    left = left.reshape(features, 2, SLOTS, LANES)
    total = total.reshape(features, 2, SLOTS, LANES)
    gl, hl = left[:, 0], left[:, 1]
    gt, ht = total[:, 0], total[:, 1]
    gain = gl * gl / (hl + 1.0)
    gain = gain + (gt - gl) ** 2 / (ht - hl + 1.0)
    gain = gain - gt * gt / (ht + 1.0)
    gain_ref[...] = gain
    best_ref[...] = jnp.max(gain, axis=0)


def per_device(bins, grads, hess, node):
    rows = bins.shape[1]
    g = grads.astype(jnp.float32).reshape(1, rows)
    h = hess.astype(jnp.float32).reshape(1, rows)
    part = local_hist(bins, node.reshape(1, rows), g, h, 8)
    hist = lax.psum_scatter(part, "row", scatter_dimension=0, tiled=True)
    features = hist.shape[0]
    gain, top = pl.pallas_call(
        gain_kernel,
        out_shape=(
            jax.ShapeDtypeStruct((features, SLOTS, LANES), jnp.float32),
            jax.ShapeDtypeStruct((SLOTS, LANES), jnp.float32),
        ),
    )(hist)
    local_best = jnp.max(top.reshape(NODES, BINS // LANES * LANES), axis=1)
    best = lax.pmax(local_best, ("row", "feat"))
    out = gain.reshape(features, NODES, BINS) - best[None, :, None]
    return out, best


def solution(mesh):
    return jax.shard_map(
        per_device,
        mesh=mesh,
        in_specs=(P("feat", "row"), P("row"), P("row"), P("row")),
        out_specs=(P(("feat", "row"), None, None), P()),
        check_vma=False,
    )
```

time: 562 us -> 199 us (0.35)
  matrix products: 400 us -> 0 us
  Pallas kernels: 0 us -> 85.8 us
  local copies, waits for them, and re-layouts: 32.7 us -> 1.12 us
  other arithmetic: 20.6 us -> 4.37 us
  waiting for transfers between devices: 38.7 us -> 54.1 us
  blocking collectives: 54.4 us -> 39.3 us
    dot_general x32 -> x0, matrix products: 400 us -> none  [block_hist(): jnp.einsum('kr,frb->fkb', weighted, onehot, preferred_element_type=jnp.fl...]
    pallas_call x0 -> x2, Pallas kernels: none -> 85.8 us  [the longest x1 82.7 us: local_hist(): pl.pallas_call(hist_kernel, grid=(features // block,), in_specs=[pl.Block...]
    eq x32 -> x0, local copies, waits for them, and re-layouts: 30.9 us -> none  [block_hist(): onehot = (columns[:, :, None] == levels[None, None, :]).astype(jnp.bfloat16)]
    another operation x3 -> x0, other arithmetic: 18.4 us -> none
    reduce_scatter x1, waiting for transfers between devices: 38.6 us -> 54 us  [per_device(): hist = lax.psum_scatter(part, 'row', scatter_dimension=0, tiled=True)]
    psum x1 -> x0, blocking collectives: 15.1 us -> none  [per_device(): node_sums = lax.psum(own_sums, 'row')]
where the time goes in v1:
time: 199 us
  Pallas kernels  85.8 us (43%)
  waiting for transfers between devices  54.1 us (27%)
  blocking collectives  39.3 us (20%)
  between operations  14 us (7%)
  other arithmetic  4.37 us (2%)
    pallas_call x1, Pallas kernels, local_hist(): pl.pallas_call(hist_kernel, grid=(features // block,), in_specs=[pl.Block...  82.7 us
    reduce_scatter x1, waiting for transfers between devices, per_device(): hist = lax.psum_scatter(part, 'row', scatter_dimension=0, tiled=True)  54 us
    pmax x1, blocking collectives, per_device(): best = lax.pmax(local_best, ('row', 'feat'))  39.3 us
  transfers between devices with their start and end apart: 1, of which 1 were waited for; matrix products, arithmetic and copies ran while one was open for 0% of the time, Pallas kernels for 0%

profile of v1, /device:TPU:0, one launch (start us, length us, event | category | flops | bytes accessed | tf_op | source)
XLA Modules:
  0.0 198.7 jit_solution(6771316736018067617)
XLA Ops:
  7.2 0.0 reduce-scatter.2.cloned.1.call-start
  7.2 1.3 reshape.29
  8.5 1.3 reshape.31
  9.9 82.7 %shard_map.59 = f32[256,32,128]{2,1,0:T(8,128)} custom-call(s32[256,8192]{1,0:T(8,128)} %bins_ref.1, s32[1,8192]{1,0:T(1,128)} %bitcast.5, f32[1,8192]{1,0:T(1,128)} %bitcast.3, f32[1,8192]{1,0:T(1,128)} %bitcast.4), custom_call_target="tpu_custom_call" | custom-call | tf_op jit(solution)/shard_map/pallas_call | solution.py:63
  92.6 0.0 reduce-scatter.2.cloned.1.call-update
  92.6 54.0 %reduce-scatter.2.cloned.1.call-done.hist_ref = f32[32,32,128]{2,1,0:T(8,128)} async-done(((f32[256,32,128]{2,1,0:T(8,128)}), f32[32,32,128]{2,1,0:T(8,128)}) %reduce-scatter.2.cloned.1.call-update) | async-done | bytes 524304 | tf_op jit(solution)/shard_map/reduce_scatter | solution.py:111
  146.7 3.1 %shard_map.60 = (f32[32,16,128]{2,1,0:T(8,128)}, f32[16,128]{1,0:T(8,128)}) custom-call(f32[32,32,128]{2,1,0:T(8,128)} %reduce-scatter.2.cloned.1.call-done.hist_ref), custom_call_target="tpu_custom_call" | custom-call | tf_op jit(solution)/shard_map/pallas_call | solution.py:113
  149.8 0.8 reduce_max.10
  150.6 0.1 reduce_max.14
  150.7 0.1 reduce_max.18
  150.8 1.0 reshape.28
  151.8 39.3 %pmax.7 = f32[8]{0:T(128)S(1)} all-reduce(f32[8]{0:T(128)S(1)} %reduce_max.18), channel_id=1, replica_groups=mesh['row'=8,'feat'=4] {'row','feat'}, use_global_device_ids=true, to_apply=%region_3.4 | all-reduce | flops 8 | bytes 64 | tf_op jit(solution)/shard_map/pmax | solution.py:121
  191.1 0.0 copy-start
  191.1 0.8 broadcast_subtract_fusion
  191.9 0.0 copy-done
Async XLA Ops:
  7.2 139.5 %reduce-scatter.2.cloned.1.call-start = ((), (), s32[]{:S(2)}) async-start(), calls=%async_computation.1 | async-start | bytes 4718592 | tf_op jit(solution)/shard_map/reduce_scatter | solution.py:111
  191.1 0.8 copy-start
Sparse Core Ops, SparseCore 0:
  92.8 53.8 reduce-scatter.1

commit v2 on v0

v2 whole, which is shorter than its diff:
```python
import functools
import jax
import jax.numpy as jnp
from jax import lax
from jax.experimental import pallas as pl
from jax.experimental.pallas import tpu as pltpu
from jax.sharding import PartitionSpec as P

BINS = 256
NODES = 8
LANES = 128
SUBLANES = 8
LOW = 64
TILE = 256
GROUP = TILE // LOW
HALVES = LANES // LOW
TOPS = BINS // LANES
SLOTS = NODES * TOPS
LINES = 2 * SLOTS
MESH = pl.DeviceIdType.MESH


def partner(me, k, n):
    if n & (n - 1):
        return (me + k) % n
    out, weight = 0, 1
    while weight < n:
        out = out + (((me // weight) % 2 + (k // weight) % 2) % 2) * weight
        weight *= 2
    return out


def kernel(
    n, m, block, chunks, bins_hbm, node_ref, g_ref, h_ref, out_ref, best_ref,
    bins_buf, high_ref, low_ref, g_all, h_all, acc_ref, stage, landed, row_best, feat_best,
    load_sem, send_sem, recv_sem, row_send, row_recv, feat_send, feat_recv,
):
    rows = bins_buf.shape[2]
    me = lax.axis_index("row")
    mine = lax.axis_index("feat")
    steps = n * chunks
    sent = (n - 1) * chunks

    def place_of(s):
        return (partner(me, n - 1 - s // chunks, n) * chunks + s % chunks) * block

    def load(s):
        start = pl.multiple_of((place_of(s) // SUBLANES) * SUBLANES, SUBLANES)
        return pltpu.make_async_copy(
            bins_hbm.at[pl.ds(start, SUBLANES), :], bins_buf.at[s % 2], load_sem.at[s % 2]
        )

    def send(s):
        k = n - 1 - s // chunks
        return pltpu.make_async_remote_copy(
            src_ref=stage.at[s],
            dst_ref=landed.at[s],
            send_sem=send_sem.at[s],
            recv_sem=recv_sem.at[s],
            device_id={"row": partner(me, k, n)},
            device_id_type=MESH,
        )

    load(0).start()
    barrier = pltpu.get_barrier_semaphore()
    for k in range(1, n):
        pl.semaphore_signal(barrier, inc=1, device_id={"row": (me + k) % n}, device_id_type=MESH)
    for k in range(1, m):
        pl.semaphore_signal(barrier, inc=1, device_id={"feat": (mine + k) % m}, device_id_type=MESH)

    g = g_ref[...].astype(jnp.float32)
    h = h_ref[...].astype(jnp.float32)
    for i in range(rows // LANES):
        cols = slice(i * LANES, (i + 1) * LANES)
        g_all[:, cols] = jnp.broadcast_to(g[i : i + 1, :], (SLOTS, LANES)).astype(jnp.bfloat16)
        h_all[:, cols] = jnp.broadcast_to(h[i : i + 1, :], (SLOTS, LANES)).astype(jnp.bfloat16)
    pl.semaphore_wait(barrier, n + m - 2)

    def step(s, carry):
        load(s).wait()

        @pl.when(s + 1 < steps)
        def _():
            load(s + 1).start()

        @pl.when((s >= 1) & (s <= sent))
        def _():
            send(s - 1).start()

        offset = 0 if block % SUBLANES == 0 else place_of(s) % SUBLANES
        bins = bins_buf[s % 2]
        half = (bins // LOW) % HALVES
        slot = (bins // LANES) * NODES + node_ref[...]
        high_ref[...] = (half * SLOTS + slot).astype(jnp.float32)
        low_ref[...] = (bins % LOW).astype(jnp.float32)
        place = lax.broadcasted_iota(jnp.int32, (SLOTS, rows), 0).astype(jnp.bfloat16)
        zero = jnp.zeros((SLOTS, rows), jnp.bfloat16)
        one = jnp.ones((SLOTS, rows), jnp.bfloat16)
        for first in range(0, block, GROUP):
            left, right = [], []
            for f in range(first, first + GROUP):
                row = pl.ds(offset + f, 1)
                high = jnp.broadcast_to(high_ref[row, :], (SLOTS, rows)).astype(jnp.bfloat16)
                low = jnp.broadcast_to(low_ref[row, :], (SLOTS, rows)).astype(jnp.bfloat16)
                for j in range(HALVES):
                    here = high == place + jnp.asarray(SLOTS * j, jnp.bfloat16)
                    left += [jnp.where(here, g_all[...], zero), jnp.where(here, h_all[...], zero)]
                for j in range(LOW // SLOTS):
                    here = low == place + jnp.asarray(SLOTS * j, jnp.bfloat16)
                    right.append(jnp.where(here, one, zero))
            acc_ref[...] = lax.dot_general(
                jnp.concatenate(left, 0),
                jnp.concatenate(right, 0),
                (((1,), (1,)), ((), ())),
                preferred_element_type=jnp.float32,
            )
            for i in range(GROUP):
                parts = []
                for j in range(HALVES):
                    top = (i * HALVES + j) * LINES
                    parts.append(acc_ref[top : top + LINES, i * LOW : (i + 1) * LOW])
                stage[s, first + i] = jnp.concatenate(parts, 1)
        return carry

    lax.fori_loop(0, steps, step, 0)

    def drain(s, carry):
        send(s).wait()
        return carry

    lax.fori_loop(0, sent, drain, 0)

    lane = lax.broadcasted_iota(jnp.int32, (block * 2 * TOPS * NODES, LANES), 1)

    def finish(c, top_gain):
        def add(k, total):
            return total + landed[k * chunks + c]

        x = lax.fori_loop(0, n - 1, add, stage[sent + c])
        x = x.reshape(block * LINES, LANES)
        shift = 1
        while shift < LANES:
            x = x + jnp.where(lane >= shift, pltpu.roll(x, shift, 1), 0.0)
            shift *= 2
        x = x.reshape(block, 2, TOPS, NODES, LANES)
        left, total = [], jnp.zeros((block, 2, NODES, LANES), jnp.float32)
        for t in range(TOPS):
            left.append(x[:, :, t] + total)
            total = total + jnp.broadcast_to(x[:, :, t, :, LANES - 1 :], total.shape)
        gt, ht = total[:, 0], total[:, 1]
        base = gt * gt / (ht + 1.0)
        for t in range(TOPS):
            gl, hl = left[t][:, 0], left[t][:, 1]
            gain = gl * gl / (hl + 1.0)
            gain = gain + (gt - gl) * (gt - gl) / (ht - hl + 1.0)
            gain = gain - base
            out_ref[pl.ds(c * block, block), :, t * LANES : (t + 1) * LANES] = gain
            top_gain = jnp.maximum(top_gain, jnp.max(gain, axis=0))
        return top_gain

    top_gain = lax.fori_loop(0, chunks, finish, jnp.full((NODES, LANES), -jnp.inf, jnp.float32))

    def exchange(value, slots, count, axis, index, sems, arrived):
        slots[0] = jnp.broadcast_to(jnp.max(value, axis=1, keepdims=True), (NODES, LANES))
        copies = []
        for k in range(1, count):
            copies.append(
                pltpu.make_async_remote_copy(
                    src_ref=slots.at[0],
                    dst_ref=slots.at[k],
                    send_sem=sems.at[k - 1],
                    recv_sem=arrived.at[k - 1],
                    device_id={axis: (index + k) % count},
                    device_id_type=MESH,
                )
            )
            copies[-1].start()
        for copy in copies:
            copy.wait()
        best = slots[0]
        for k in range(1, count):
            best = jnp.maximum(best, slots[k])
        return best

    best = exchange(top_gain, row_best, n, "row", me, row_send, row_recv)
    best = exchange(best, feat_best, m, "feat", mine, feat_send, feat_recv)
    best_ref[...] = best
    for t in range(TOPS):
        cols = slice(t * LANES, (t + 1) * LANES)
        out_ref[:, :, cols] = out_ref[:, :, cols] - best[None]


def solution(mesh):
    n, m = mesh.shape["row"], mesh.shape["feat"]

    def per_device(bins, grads, hess, node):
        features, rows = bins.shape
        own = features // n
        block = min(own, SUBLANES)
        chunks = own // block
        vmem = pl.BlockSpec(memory_space=pltpu.VMEM)
        piece = (block, LINES, LANES)
        out, best = pl.pallas_call(
            functools.partial(kernel, n, m, block, chunks),
            in_specs=[pl.BlockSpec(memory_space=pl.ANY), vmem, vmem, vmem],
            out_specs=(vmem, vmem),
            out_shape=(
                jax.ShapeDtypeStruct((own, NODES, BINS), jnp.float32),
                jax.ShapeDtypeStruct((NODES, LANES), jnp.float32),
            ),
            scratch_shapes=[
                pltpu.VMEM((2, SUBLANES, rows), jnp.int32),
                pltpu.VMEM((SUBLANES, rows), jnp.float32),
                pltpu.VMEM((SUBLANES, rows), jnp.float32),
                pltpu.VMEM((SLOTS, rows), jnp.bfloat16),
                pltpu.VMEM((SLOTS, rows), jnp.bfloat16),
                pltpu.VMEM((GROUP * HALVES * LINES, TILE), jnp.float32),
                pltpu.VMEM((n * chunks,) + piece, jnp.float32),
                pltpu.VMEM(((n - 1) * chunks,) + piece, jnp.float32),
                pltpu.VMEM((n, NODES, LANES), jnp.float32),
                pltpu.VMEM((m, NODES, LANES), jnp.float32),
                pltpu.SemaphoreType.DMA((2,)),
                pltpu.SemaphoreType.DMA(((n - 1) * chunks,)),
                pltpu.SemaphoreType.DMA(((n - 1) * chunks,)),
                pltpu.SemaphoreType.DMA((n - 1,)),
                pltpu.SemaphoreType.DMA((n - 1,)),
                pltpu.SemaphoreType.DMA((m - 1,)),
                pltpu.SemaphoreType.DMA((m - 1,)),
            ],
            compiler_params=pltpu.CompilerParams(
                collective_id=0, has_side_effects=True, vmem_limit_bytes=56 << 20
            ),
        )(bins, node.reshape(1, rows), grads.reshape(-1, LANES), hess.reshape(-1, LANES))
        return out, best[:, 0]

    return jax.shard_map(
        per_device,
        mesh=mesh,
        in_specs=(P("feat", "row"), P("row"), P("row"), P("row")),
        out_specs=(P(("feat", "row"), None, None), P()),
        check_vma=False,
    )
```

time: 562 us -> 104 us (0.19)
  matrix products: 400 us -> 0 us
  Pallas kernels: 0 us -> 99.7 us
  blocking collectives: 54.4 us -> 0 us
  waiting for transfers between devices: 38.7 us -> 0 us
  local copies, waits for them, and re-layouts: 32.7 us -> 2.97 us
  other arithmetic: 20.6 us -> 0 us
  between operations: 14.1 us -> 0.64 us
    dot_general x32 -> x0, matrix products: 400 us -> none  [block_hist(): jnp.einsum('kr,frb->fkb', weighted, onehot, preferred_element_type=jnp.fl...]
    pallas_call x0 -> x1, Pallas kernels: none -> 99.7 us  [per_device(): pl.pallas_call(functools.partial(kernel, n, m, block, chunks), in_specs=[...]
    pmax x1 -> x0, blocking collectives: 39.3 us -> none  [per_device(): best = lax.pmax(local_best, ('row', 'feat'))]
    reduce_scatter x1 -> x0, waiting for transfers between devices: 38.6 us -> none  [per_device(): lax.psum_scatter(partial_hist, 'row', scatter_dimension=0, tiled=True)]
    eq x32 -> x0, local copies, waits for them, and re-layouts: 30.9 us -> none  [block_hist(): onehot = (columns[:, :, None] == levels[None, None, :]).astype(jnp.bfloat16)]
    another operation x3 -> x0, other arithmetic: 18.4 us -> none
    psum x1 -> x0, blocking collectives: 15.1 us -> none  [per_device(): node_sums = lax.psum(own_sums, 'row')]
  transfers between devices with their start and end apart: 1 -> 0, of which waited for: 1 -> 0; matrix products, arithmetic and copies ran while one was open for 0% -> 0% of each run, Pallas kernels for 0% -> 0%
where the time goes in v2:
time: 104 us; the launch traced here: 103 us
  Pallas kernels  99.7 us (96%)
  local copies, waits for them, and re-layouts  2.97 us (3%)
    pallas_call x1, Pallas kernels, per_device(): pl.pallas_call(functools.partial(kernel, n, m, block, chunks), in_specs=[...  99.7 us

profile of v2, /device:TPU:0, one launch (start us, length us, event | category | flops | bytes accessed | tf_op | source)
XLA Modules:
  0.0 103.4 jit_solution(6041475689814032797)
XLA Ops:
  0.6 99.7 %shard_map.59 = (f32[32,8,256]{2,1,0:T(8,128)}, f32[8,128]{1,0:T(8,128)}) custom-call(s32[256,8192]{1,0:T(8,128)} %bins_hbm.1, s32[1,8192]{1,0:T(1,128)} %bitcast.3, bf16[64,128]{1,0:T(8,128)(2,1)} %bitcast.4, bf16[64,128]{1,0:T(8,128)(2,1)} %bitcast.5), custom_call_target="tpu_custom_call" | custom-call | tf_op jit(solution)/shard_map/pallas_call | solution.py:203
  100.4 1.3 %slice_reduce_fusion = f32[8]{0:T(128)} fusion(f32[8,128]{1,0:T(8,128)} %get-tuple-element.5), kind=kLoop, calls=%fused_computation | loop fusion | bytes 64 | tf_op jit(solution)/shard_map/slice | solution.py:234
  101.7 1.7 %copy.7 = f32[32,8,256]{2,1,0:T(8,128)} copy(f32[32,8,256]{2,1,0:T(8,128)} %get-tuple-element.8) | data formatting | bytes 524288

commit v3 on v2

--- a/solution.py
+++ b/solution.py
@@ -47,7 +47,7 @@
     def load(s):
         start = pl.multiple_of((place_of(s) // SUBLANES) * SUBLANES, SUBLANES)
         return pltpu.make_async_copy(
-            bins_hbm.at[pl.ds(start, SUBLANES), :], bins_buf.at[s % 2], load_sem.at[s % 2]
+            bins_hbm.at[pl.ds(start, bins_buf.shape[1]), :], bins_buf.at[s % 2], load_sem.at[s % 2]
         )
 
     def send(s):
@@ -89,10 +89,12 @@
 
         offset = 0 if block % SUBLANES == 0 else place_of(s) % SUBLANES
         bins = bins_buf[s % 2]
-        half = (bins // LOW) % HALVES
-        slot = (bins // LANES) * NODES + node_ref[...]
-        high_ref[...] = (half * SLOTS + slot).astype(jnp.float32)
-        low_ref[...] = (bins % LOW).astype(jnp.float32)
+        upper = bins >= LANES
+        rest = jnp.where(upper, bins - LANES, bins)
+        second = rest >= LOW
+        slot = node_ref[...] + jnp.where(upper, NODES, 0)
+        high_ref[...] = jnp.where(second, slot + SLOTS, slot).astype(jnp.float32)
+        low_ref[...] = jnp.where(second, rest - LOW, rest).astype(jnp.float32)
         place = lax.broadcasted_iota(jnp.int32, (SLOTS, rows), 0).astype(jnp.bfloat16)
         zero = jnp.zeros((SLOTS, rows), jnp.bfloat16)
         one = jnp.ones((SLOTS, rows), jnp.bfloat16)
@@ -184,10 +186,10 @@
 
     best = exchange(top_gain, row_best, n, "row", me, row_send, row_recv)
     best = exchange(best, feat_best, m, "feat", mine, feat_send, feat_recv)
-    best_ref[...] = best
-    for t in range(TOPS):
-        cols = slice(t * LANES, (t + 1) * LANES)
-        out_ref[:, :, cols] = out_ref[:, :, cols] - best[None]
+    across = lax.broadcasted_iota(jnp.int32, (NODES, LANES), 1)
+    down = lax.broadcasted_iota(jnp.int32, (NODES, LANES), 0)
+    flat = jnp.max(jnp.where(across == down, best, -jnp.inf), axis=0, keepdims=True)
+    best_ref[...] = flat[:, :NODES]
 
 
 def solution(mesh):
@@ -196,7 +198,8 @@
     def per_device(bins, grads, hess, node):
         features, rows = bins.shape
         own = features // n
-        block = min(own, SUBLANES)
+        block = own if own < SUBLANES else next(b for b in (2 * SUBLANES, SUBLANES) if own % b == 0)
+        held = max(block, SUBLANES)
         chunks = own // block
         vmem = pl.BlockSpec(memory_space=pltpu.VMEM)
         piece = (block, LINES, LANES)
@@ -206,12 +209,12 @@
             out_specs=(vmem, vmem),
             out_shape=(
                 jax.ShapeDtypeStruct((own, NODES, BINS), jnp.float32),
-                jax.ShapeDtypeStruct((NODES, LANES), jnp.float32),
+                jax.ShapeDtypeStruct((1, NODES), jnp.float32),
             ),
             scratch_shapes=[
-                pltpu.VMEM((2, SUBLANES, rows), jnp.int32),
-                pltpu.VMEM((SUBLANES, rows), jnp.float32),
-                pltpu.VMEM((SUBLANES, rows), jnp.float32),
+                pltpu.VMEM((2, held, rows), jnp.int32),
+                pltpu.VMEM((held, rows), jnp.float32),
+                pltpu.VMEM((held, rows), jnp.float32),
                 pltpu.VMEM((SLOTS, rows), jnp.bfloat16),
                 pltpu.VMEM((SLOTS, rows), jnp.bfloat16),
                 pltpu.VMEM((GROUP * HALVES * LINES, TILE), jnp.float32),
@@ -231,7 +234,8 @@
                 collective_id=0, has_side_effects=True, vmem_limit_bytes=56 << 20
             ),
         )(bins, node.reshape(1, rows), grads.reshape(-1, LANES), hess.reshape(-1, LANES))
-        return out, best[:, 0]
+        best = best.reshape(NODES)
+        return out - best[None, :, None], best
 
     return jax.shard_map(
         per_device,

time: 104 us -> 94.5 us (0.909)
  Pallas kernels: 99.7 us -> 90.7 us
  local copies, waits for them, and re-layouts: 2.97 us -> 1.13 us
  other arithmetic: 0 us -> 1.74 us
    pallas_call x1, Pallas kernels: 99.7 us -> 90.7 us  [per_device(): pl.pallas_call(functools.partial(kernel, n, m, block, chunks), in_specs=[...]
    sub x0 -> x1, other arithmetic: none -> 1.74 us  [per_device(): return (out - best[None, :, None], best)]
    slice x1 -> x0, local copies, waits for them, and re-layouts: 1.3 us -> none  [per_device(): return (out, best[:, 0])]
where the time goes in v3:
time: 94.5 us; the launch traced here: 94.2 us
  Pallas kernels  90.7 us (96%)
  other arithmetic  1.74 us (2%)
  local copies, waits for them, and re-layouts  1.13 us (1%)
    pallas_call x1, Pallas kernels, per_device(): pl.pallas_call(functools.partial(kernel, n, m, block, chunks), in_specs=[...  90.7 us

profile of v3, /device:TPU:0, one launch (start us, length us, event | category | flops | bytes accessed | tf_op | source)
XLA Modules:
  0.0 94.2 jit_solution(16406904534879633901)
XLA Ops:
  0.6 90.7 %shard_map.59 = (f32[32,8,256]{2,1,0:T(8,128)}, f32[1,8]{1,0:T(1,128)}) custom-call(s32[256,8192]{1,0:T(8,128)} %bins_hbm.1, s32[1,8192]{1,0:T(1,128)} %bitcast.4, bf16[64,128]{1,0:T(8,128)(2,1)} %bitcast.5, bf16[64,128]{1,0:T(8,128)(2,1)} %bitcast.6), custom_call_target="tpu_custom_call" | custom-call | tf_op jit(solution)/shard_map/pallas_call | solution.py:206
  91.3 1.7 %broadcast_subtract_fusion = f32[32,8,256]{2,1,0:T(8,128)} fusion(f32[32,8,256]{2,1,0:T(8,128)} %get-tuple-element.4, f32[8]{0:T(128)} %bitcast.7), kind=kLoop, calls=%fused_computation | loop fusion | flops 65536 | bytes 524320 | tf_op jit(solution)/shard_map/sub | solution.py:238
  93.0 1.1 %copy.7 = f32[8]{0:T(128)} copy(f32[8]{0:T(128)} %bitcast.8) | data formatting | bytes 64
